TPU v7x, 32 devices: a whole 2x2x4 slice. The times are simulated.
32 devices in a mesh: row: 4 (over x, core), col: 8 (over z, y).
Axes of the slice: x: 2, y: 2, z: 4, core: 2. Of those that a mesh axis runs over, the one named last changes fastest.
Arguments:
- front_matrix: float32 [32, 4, 128, 16, 8, 128], P(None, 'row', None, None, 'col'), as said below
- children: bfloat16 [2, 4, 4, 128, 16, 8, 128], P(None, None, 'row', None, None, 'col'), may hold values from -0.5 to 0.5
- child_map: int32 [2, 16], replicated, may hold values from 0 to 127, as said below
- row_order: int32 [2, 16, 128], replicated, may hold values from 0 to 127, each once within a row
Outputs:
- schur_part: float32 [32, 4, 128, 16, 8, 128], P(None, 'row', None, None, 'col')
- factor_part: float32 [32, 4, 128, 1536], P('col', 'row')
Inputs may be any that keep to these rules, and one draw needn't show every extreme that they name: `front_matrix`: Off-diagonal entries lie within -1.2 and 1.2 + 0.3 * sqrt(16384); diagonal entries lie between 2.5 and 3.9 times the square root of 16384. The lower triangle, with the children's rows added and mirrored, is positive definite. `child_map`: each child sends its tile rows to distinct front tile rows. Of the 4 tile rows of one child held by one device row, at most 2 go to any one device row (front tile row modulo 4), and exactly 2 go to some device row.
All inputs are finite; a program needn't handle non-finite values.
Results may differ from a plain program's by a relative error of at most 0.001.
Values may be sent and summed in bfloat16 or wider, within the bound.
No kernel may reach another device: no remote copies, remote signals or barrier semaphores. Data moves between devices by JAX's collectives and lax.ppermute only.
A program may use at most 384 MiB of HBM per device.

v0:
```python
import jax
import jax.numpy as jnp
from jax import lax
from jax.sharding import PartitionSpec as P

PWT = 4
STEPS = 3
CAP = 2


def from_root(value, axis, source):
    kept = jnp.where(lax.axis_index(axis) == source, value, 0).astype(value.dtype)
    return lax.psum(kept, axis)


def slot_ranks(mapping, row_count):
    indices = jnp.arange(mapping.shape[0], dtype=jnp.int32)
    sources = indices % row_count
    targets = mapping % row_count
    earlier = (
        (sources[:, None] == sources[None, :])
        & (targets[:, None] == targets[None, :])
        & (indices[None, :] < indices[:, None])
    )
    return (sources, targets, jnp.sum(earlier.astype(jnp.int32), axis=1))


def pack_child(rows_local, ordering, targets, rank_in_group, row_count, row_dev):
    local_count, tile_size, width_local = rows_local.shape
    own_ids = jnp.arange(local_count, dtype=jnp.int32) * row_count + row_dev
    own_order = ordering[own_ids]
    onehot_rows = (
        own_order[:, :, None] == jnp.arange(tile_size, dtype=jnp.int32)[None, None, :]
    ).astype(jnp.bfloat16)
    moved_rows = jnp.einsum(
        "atr,atx->arx", onehot_rows, rows_local, preferred_element_type=jnp.float32
    ).astype(jnp.bfloat16)
    slot_of = targets[own_ids] * CAP + rank_in_group[own_ids]
    selector = (jnp.arange(row_count * CAP, dtype=jnp.int32)[:, None] == slot_of[None, :]).astype(
        jnp.bfloat16
    )
    packed = jnp.einsum(
        "ja,arx->jrx", selector, moved_rows, preferred_element_type=jnp.float32
    ).astype(jnp.bfloat16)
    return packed.reshape(row_count, CAP, tile_size, width_local)


def unpack_selector(mapping, sources, targets, rank_in_group, row_count, row_dev, local_rows):
    slot_of = sources * CAP + rank_in_group
    landing = (
        (mapping // row_count)[:, None] == jnp.arange(local_rows, dtype=jnp.int32)[None, :]
    ) & (targets == row_dev)[:, None]
    arrival = slot_of[:, None] == jnp.arange(row_count * CAP, dtype=jnp.int32)[None, :]
    return jnp.dot(
        landing.astype(jnp.bfloat16).T,
        arrival.astype(jnp.bfloat16),
        preferred_element_type=jnp.float32,
    ).astype(jnp.bfloat16)


def place_rows(matrix_rows, selector, received):
    flat_slots = received.reshape(selector.shape[1], received.shape[2], received.shape[3])
    return matrix_rows + jnp.einsum(
        "aj,jtx->atx", selector, flat_slots, preferred_element_type=jnp.float32
    )


def current_tile(matrix, factors, copies, local_col, tile_size):
    owned = matrix[:, :, local_col * tile_size : (local_col + 1) * tile_size]
    for earlier_index in range(len(factors)):
        owned = owned - jnp.einsum(
            "atk,uk->atu",
            factors[earlier_index],
            copies[earlier_index][local_col],
            precision=lax.Precision.HIGHEST,
            preferred_element_type=jnp.float32,
        )
    return owned


def shards(front_matrix, children, child_map, row_order):
    row_count = lax.axis_size("row")
    col_count = lax.axis_size("col")
    row_dev = lax.axis_index("row")
    col_dev = lax.axis_index("col")
    local_rows = front_matrix.shape[0]
    tile_size = front_matrix.shape[2]
    local_cols = front_matrix.shape[3]
    width_local = local_cols * tile_size
    panel_width = PWT * tile_size
    matrix = front_matrix.reshape(local_rows, tile_size, width_local)
    packed = []
    selectors = []
    for child_index in range(2):
        sources, targets, rank_in_group = slot_ranks(child_map[child_index], row_count)
        rows_local = children[child_index].reshape(children.shape[1], tile_size, width_local)
        packed.append(
            pack_child(
                rows_local, row_order[child_index], targets, rank_in_group, row_count, row_dev
            )
        )
        selectors.append(
            unpack_selector(
                child_map[child_index],
                sources,
                targets,
                rank_in_group,
                row_count,
                row_dev,
                local_rows,
            )
        )
    received = (
        lax.all_to_all(packed[0], "row", split_axis=0, concat_axis=0, tiled=True),
        lax.all_to_all(packed[1], "row", split_axis=0, concat_axis=0, tiled=True),
    )
    for child_index in range(2):
        matrix = place_rows(matrix, selectors[child_index], received[child_index])
    pending = []
    row_tiles = jnp.arange(local_rows, dtype=jnp.int32) * row_count + row_dev
    col_tiles = jnp.arange(local_cols, dtype=jnp.int32) * col_count + col_dev
    factors = []
    copies = []
    for panel_index in range(STEPS):
        first_tile = panel_index * PWT
        pieces = []
        for offset in range(PWT):
            tile_col = first_tile + offset
            local_col = tile_col // col_count
            owned = current_tile(matrix, factors, copies, local_col, tile_size)
            pieces.append(from_root(owned, "col", tile_col % col_count))
        panel_cols = jnp.concatenate(pieces, axis=2)
        blocks = []
        for offset in range(PWT):
            tile_row = first_tile + offset
            blocks.append(from_root(panel_cols[tile_row // row_count], "row", tile_row % row_count))
        diagonal = jnp.concatenate(blocks, axis=0)
        mirrored = jnp.tril(diagonal) + jnp.tril(diagonal, -1).T
        cholesky_factor = jnp.linalg.cholesky(mirrored)
        flat_cols = panel_cols.reshape(local_rows * tile_size, panel_width)
        solved = jax.scipy.linalg.solve_triangular(
            cholesky_factor, flat_cols.T, lower=True
        ).T.reshape(local_rows, tile_size, panel_width)
        diag_rows = cholesky_factor.reshape(PWT, tile_size, panel_width)[
            jnp.clip(row_tiles - first_tile, 0, PWT - 1)
        ]
        inside = (row_tiles >= first_tile) & (row_tiles < first_tile + PWT)
        factor = jnp.where(inside[:, None, None], diag_rows, solved)
        factor = jnp.where((row_tiles < first_tile)[:, None, None], jnp.zeros_like(factor), factor)
        picked = factor[col_tiles // row_count]
        factor_cols = from_root(picked.astype(jnp.bfloat16), "row", col_dev % row_count).astype(
            picked.dtype
        )
        factors.append(factor)
        copies.append(factor_cols)
    stacked = jnp.concatenate(factors, axis=2)
    stacked_cols = jnp.concatenate(copies, axis=2)
    update = jnp.einsum(
        "atk,buk->atbu",
        stacked,
        stacked_cols,
        precision=lax.Precision.HIGHEST,
        preferred_element_type=jnp.float32,
    )
    final_rows = matrix.reshape(local_rows, tile_size, local_cols, tile_size) - update
    kept_mask = (row_tiles[:, None] >= col_tiles[None, :]) & (col_tiles[None, :] >= STEPS * PWT)
    schur_part = jnp.where(
        kept_mask[:, None, :, None], final_rows, jnp.zeros_like(final_rows)
    ).reshape(front_matrix.shape)
    share_rows = local_rows // col_count
    factor_part = lax.dynamic_slice_in_dim(stacked, col_dev * share_rows, share_rows, 0).reshape(
        share_rows, 1, tile_size, STEPS * panel_width
    )
    return (schur_part, factor_part)


def solution(mesh):
    placed = (
        P(None, "row", None, None, "col", None),
        P(None, None, "row", None, None, "col", None),
        P(),
        P(),
    )
    return jax.shard_map(
        shards,
        mesh=mesh,
        in_specs=placed,
        out_specs=(P(None, "row", None, None, "col", None), P("col", "row", None, None)),
        check_vma=False,
    )
```

profile of v0, /device:TPU:0, one launch (start us, length us, event | category | flops | bytes accessed | tf_op | source)
XLA Modules:
  0.0 2242.3 jit_solution(8669075045916751442)
XLA Ops:
  67.1 24.8 %all-to-all-done.1 = bf16[4,2,128,2048]{3,1,2,0:T(2,128)(2,1)} async-done(((bf16[4,2,128,2048]{3,1,2,0:T(2,128)(2,1)}), bf16[4,2,128,2048]{3,1,2,0:T(2,128)(2,1)}, u32[]{:S(2)}, u32[]{:S(2)}) %all-to-all-start.1) | async-done | bytes 4194336 | tf_op jit(solution)/shard_map/all_to_all | solution.py:115
  97.4 92.9 %reduce.19 = f32[32,128,16,128]{3,2,1,0:T(8,128)} reduce(f32[32,1,128,16,1,128]{5,4,3,2,1,0:T(1,128)} %param.7, f32[]{:T(128)} %broadcast.1002), dimensions={1,4}, to_apply=%param.7.reduce_sub_computation.3 | reduce | bytes 67108864 | tf_op args[0]
  190.3 35.5 %reshape.502 = f32[32,128,2048]{2,1,0:T(8,128)} reshape(f32[32,128,16,128]{3,2,1,0:T(8,128)} %reduce.19) | data formatting | bytes 67108864 | tf_op jit(solution)/shard_map/reshape | solution.py:91
  259.0 15.9 fusion.63
  274.9 14.9 fusion.64
  289.8 67.2 %copy_add_fusion = f32[32,128,2048]{2,1,0:T(8,128)} fusion(f32[32,128,2048]{2,0,1:T(8,128)} %fusion.63, f32[32,128,2048]{2,1,0:T(8,128)} %reshape.502, f32[32,128,2048]{2,0,1:T(8,128)} %fusion.64), kind=kLoop, calls=%fused_computation.21 | loop fusion | flops 16777216 | bytes 134217728 | tf_op jit(solution)/shard_map/add | solution.py:63
  362.5 275.0 %all-reduce.27.cloned.1.call-done = (f32[32,128,128]{2,1,0:T(8,128)}, f32[32,128,128]{2,1,0:T(8,128)}, f32[32,128,128]{2,1,0:T(8,128)}, f32[32,128,128]{2,1,0:T(8,128)}) async-done(((f32[32,128,128]{2,1,0:T(8,128)}, f32[32,128,128]{2,1,0:T(8,128)}, f32[32,128,128]{2,1,0:T(8,128)}, f32[32,128,128]{2,1,0:T(8,128)}), (f32[32,128,128]{2,1,0:T(8,128)}, f32[32,128,128]{2,1,0:T(8,128)}, f32[32,128,128]{2,1,0:T(8,128)}, ...) | async-done | bytes 8388624 | tf_op jit(solution)/shard_map/psum | solution.py:13
  657.0 26.2 %all-reduce.33.cloned.1.call-done = (f32[128,512]{1,0:T(8,128)}, f32[128,512]{1,0:T(8,128)}, f32[128,512]{1,0:T(8,128)}, f32[128,512]{1,0:T(8,128)}) async-done(((f32[128,512]{1,0:T(8,128)}, f32[128,512]{1,0:T(8,128)}, f32[128,512]{1,0:T(8,128)}, f32[128,512]{1,0:T(8,128)}), (f32[128,512]{1,0:T(8,128)}, f32[128,512]{1,0:T(8,128)}, f32[128,512]{1,0:T(8,128)}, ...) | async-done | bytes 1048592 | tf_op jit(solution)/shard_map/psum | solution.py:13
  688.2 11.7 cholesky.374
  710.5 11.7 cholesky.393
  733.2 11.7 cholesky.414
  755.4 11.8 cholesky.431
  794.4 39.3 %custom-call.34 = f32[4,128,128]{1,2,0:T(8,128)S(1)} custom-call(f32[4,128,128]{2,1,0:T(8,128)S(1)} %get-tuple-element.24), custom_call_target="InvertDiagBlocksLowerTriangular" | custom-call | tf_op jit(solution)/shard_map/jit(_solve_triangular)/triangular_solve | solution.py:141
  871.9 11.8 select_select_fusion.4
  911.0 32.4 %all-reduce.17.cloned.1.call-done = bf16[16,128,512]{2,1,0:T(8,128)(2,1)} async-done(((bf16[16,128,512]{2,1,0:T(8,128)(2,1)}), bf16[16,128,512]{2,1,0:T(8,128)(2,1)}) %all-reduce.17.cloned.1.call-update) | async-done | bytes 2097168 | tf_op jit(solution)/shard_map/psum | solution.py:13
  954.9 272.6 %all-reduce.25.cloned.1.call-done = (f32[32,128,128]{2,1,0:T(8,128)}, f32[32,128,128]{2,1,0:T(8,128)}, f32[32,128,128]{2,1,0:T(8,128)}, f32[32,128,128]{2,1,0:T(8,128)}) async-done(((f32[32,128,128]{2,1,0:T(8,128)}, f32[32,128,128]{2,1,0:T(8,128)}, f32[32,128,128]{2,1,0:T(8,128)}, f32[32,128,128]{2,1,0:T(8,128)}), (f32[32,128,128]{2,1,0:T(8,128)}, f32[32,128,128]{2,1,0:T(8,128)}, f32[32,128,128]{2,1,0:T(8,128)}, ...) | async-done | bytes 8388624 | tf_op jit(solution)/shard_map/psum | solution.py:13
  1255.3 17.9 all-reduce.31.cloned.1.call-done
  1278.2 11.7 cholesky.446
  1300.6 11.7 cholesky.465
  1323.2 11.7 cholesky.486
  1345.3 11.9 cholesky.503
  1384.2 39.3 %custom-call.38 = f32[4,128,128]{1,2,0:T(8,128)S(1)} custom-call(f32[4,128,128]{2,1,0:T(8,128)S(1)} %get-tuple-element.25), custom_call_target="InvertDiagBlocksLowerTriangular" | custom-call | tf_op jit(solution)/shard_map/jit(_solve_triangular)/triangular_solve | solution.py:141
  1461.8 12.0 select_select_fusion.2
  1500.1 33.3 %all-reduce.19.cloned.1.call-done = bf16[16,128,512]{2,1,0:T(8,128)(2,1)} async-done(((bf16[16,128,512]{2,1,0:T(8,128)(2,1)}), bf16[16,128,512]{2,1,0:T(8,128)(2,1)}) %all-reduce.19.cloned.1.call-update) | async-done | bytes 2097168 | tf_op jit(solution)/shard_map/psum | solution.py:13
  1545.3 272.2 %all-reduce.23.cloned.1.call-done = (f32[32,128,128]{2,1,0:T(8,128)}, f32[32,128,128]{2,1,0:T(8,128)}, f32[32,128,128]{2,1,0:T(8,128)}, f32[32,128,128]{2,1,0:T(8,128)}) async-done(((f32[32,128,128]{2,1,0:T(8,128)}, f32[32,128,128]{2,1,0:T(8,128)}, f32[32,128,128]{2,1,0:T(8,128)}, f32[32,128,128]{2,1,0:T(8,128)}), (f32[32,128,128]{2,1,0:T(8,128)}, f32[32,128,128]{2,1,0:T(8,128)}, f32[32,128,128]{2,1,0:T(8,128)}, ...) | async-done | bytes 8388624 | tf_op jit(solution)/shard_map/psum | solution.py:13
  1837.0 26.2 %all-reduce.29.cloned.1.call-done = (f32[128,512]{1,0:T(8,128)}, f32[128,512]{1,0:T(8,128)}, f32[128,512]{1,0:T(8,128)}, f32[128,512]{1,0:T(8,128)}) async-done(((f32[128,512]{1,0:T(8,128)}, f32[128,512]{1,0:T(8,128)}, f32[128,512]{1,0:T(8,128)}, f32[128,512]{1,0:T(8,128)}), (f32[128,512]{1,0:T(8,128)}, f32[128,512]{1,0:T(8,128)}, f32[128,512]{1,0:T(8,128)}, ...) | async-done | bytes 1048592 | tf_op jit(solution)/shard_map/psum | solution.py:13
  1935.5 11.9 cholesky.575
  1960.9 39.3 %custom-call.42 = f32[4,128,128]{1,2,0:T(8,128)S(1)} custom-call(f32[4,128,128]{2,1,0:T(8,128)S(1)} %get-tuple-element.26), custom_call_target="InvertDiagBlocksLowerTriangular" | custom-call | tf_op jit(solution)/shard_map/jit(_solve_triangular)/triangular_solve | solution.py:141
  2040.2 12.1 select_select_fusion
  2069.7 40.1 %all-reduce.21.cloned.1.call-done = bf16[16,128,512]{2,1,0:T(8,128)(2,1)} async-done(((bf16[16,128,512]{2,1,0:T(8,128)(2,1)}), bf16[16,128,512]{2,1,0:T(8,128)(2,1)}) %all-reduce.21.cloned.1.call-update) | async-done | bytes 2097168 | tf_op jit(solution)/shard_map/psum | solution.py:13
  2109.8 87.0 %fusion.1 = f32[32,1,128,16,1,128]{5,2,3,0,4,1:T(8,128)} fusion(pred[32,16]{1,0:T(8,128)(4,1)S(1)} %compare_and_fusion, bf16[16,128,512]{2,1,0:T(8,128)(2,1)} %all-reduce.21.cloned.1.call-done, bf16[16,128,512]{2,1,0:T(8,128)(2,1)} %all-reduce.19.cloned.1.call-done, bf16[16,128,512]{2,1,0:T(8,128)(2,1)S(1)} %copy-done.19, ...), kind=kOutput, calls=%fused_computation.20 | convolution fusion | flops 154667057152 | bytes 98566656 | tf_op jit(solution)/shard_map/atk,buk->atbu/dot_general | solution.py:158
  2196.8 38.6 %copy.107 = f32[32,1,128,16,1,128]{5,4,3,2,1,0:T(1,128)} copy(f32[32,1,128,16,1,128]{5,2,3,0,4,1:T(8,128)} %fusion.1) | data formatting | bytes 67108864
  (323 shorter events, 611.0 us)
Async XLA Ops:
  13.7 2.8 copy-start.20
  38.0 53.9 %all-to-all-start.1 = ((bf16[4,2,128,2048]{3,1,2,0:T(2,128)(2,1)}), bf16[4,2,128,2048]{3,1,2,0:T(2,128)(2,1)}, u32[]{:S(2)}, u32[]{:S(2)}) async-start(bf16[4,2,128,2048]{3,1,2,0:T(2,128)(2,1)} %copy.83), calls=%async_computation.1 | async-start | bytes 8388608 | tf_op jit(solution)/shard_map/all_to_all | solution.py:115
  91.9 150.5 %all-to-all-start = ((bf16[4,2,128,2048]{3,1,2,0:T(2,128)(2,1)}), bf16[4,2,128,2048]{3,1,2,0:T(2,128)(2,1)}, u32[]{:S(2)}, u32[]{:S(2)}) async-start(bf16[4,2,128,2048]{3,1,2,0:T(2,128)(2,1)} %copy.79), calls=%async_computation | async-start | bytes 8388608 | tf_op jit(solution)/shard_map/all_to_all | solution.py:114
  96.8 540.7 %all-reduce.27.cloned.1.call-start = ((), (), s32[]{:S(2)}) async-start(), calls=%async_computation.7 | async-start | bytes 16777216 | tf_op jit(solution)/shard_map/psum | solution.py:13
  190.3 35.5 %copy-start.21 = (s32[2,16]{1,0:T(2,128)S(1)}, s32[2,16]{1,0:T(2,128)}, u32[]{:S(2)}) copy-start(s32[2,16]{1,0:T(2,128)} %param.9) | copy-start | bytes 388
  362.3 320.8 %all-reduce.33.cloned.1.call-start = ((), (), s32[]{:S(2)}) async-start(), calls=%async_computation.10 | async-start | bytes 2097152 | tf_op jit(solution)/shard_map/psum | solution.py:13
  637.5 2.2 copy-start.12
  639.7 1.6 copy-start.11
  641.3 1.6 copy-start.10
  643.2 3.4 copy-start.6
  647.6 295.8 %all-reduce.17.cloned.1.call-start = ((), (), s32[]{:S(2)}) async-start(), calls=%async_computation.2 | async-start | bytes 4194304 | tf_op jit(solution)/shard_map/psum | solution.py:13
  842.7 15.1 copy-start
  849.4 8.5 copy-start.2
  857.9 1.3 copy-start.4
  892.2 335.3 %all-reduce.25.cloned.1.call-start = ((), (), s32[]{:S(2)}) async-start(), calls=%async_computation.6 | async-start | bytes 16777216 | tf_op jit(solution)/shard_map/psum | solution.py:13
  954.7 318.5 %all-reduce.31.cloned.1.call-start = ((), (), s32[]{:S(2)}) async-start(), calls=%async_computation.9 | async-start | bytes 2097152 | tf_op jit(solution)/shard_map/psum | solution.py:13
  1227.5 2.2 copy-start.18
  1229.7 1.6 copy-start.17
  1231.3 1.6 copy-start.16
  1233.2 3.4 copy-start.7
  1237.6 295.8 %all-reduce.19.cloned.1.call-start = ((), (), s32[]{:S(2)}) async-start(), calls=%async_computation.3 | async-start | bytes 4194304 | tf_op jit(solution)/shard_map/psum | solution.py:13
  1432.5 15.3 copy-start.1
  1439.2 8.6 copy-start.3
  1482.3 335.3 %all-reduce.23.cloned.1.call-start = ((), (), s32[]{:S(2)}) async-start(), calls=%async_computation.5 | async-start | bytes 16777216 | tf_op jit(solution)/shard_map/psum | solution.py:13
  1490.9 42.6 %copy-start.9 = (f32[32,128,128]{2,1,0:T(8,128)S(1)}, f32[32,128,128]{2,1,0:T(8,128)}, u32[]{:S(2)}) copy-start(f32[32,128,128]{2,1,0:T(8,128)} %fusion.83) | copy-start | bytes 6291460
  1544.7 318.5 %all-reduce.29.cloned.1.call-start = ((), (), s32[]{:S(2)}) async-start(), calls=%async_computation.8 | async-start | bytes 2097152 | tf_op jit(solution)/shard_map/psum | solution.py:13
  1817.5 2.2 copy-start.15
  1819.8 1.6 copy-start.14
  1821.3 1.6 copy-start.13
  1823.2 3.4 copy-start.8
  1827.6 282.1 %all-reduce.21.cloned.1.call-start = ((), (), s32[]{:S(2)}) async-start(), calls=%async_computation.4 | async-start | bytes 4194304 | tf_op jit(solution)/shard_map/psum | solution.py:13
  2067.8 42.0 %copy-start.19 = (bf16[16,128,512]{2,1,0:T(8,128)(2,1)S(1)}, bf16[16,128,512]{2,1,0:T(8,128)(2,1)}, u32[]{:S(2)}) copy-start(bf16[16,128,512]{2,1,0:T(8,128)(2,1)} %all-reduce.17.cloned.1.call-done) | copy-start | bytes 6291460
  (1 other events, 1.3 us)
Sparse Core Ops, SparseCore 0:
  362.4 274.9 all-reduce.26
  647.7 35.3 all-reduce.32
  892.4 51.0 all-reduce.16
  954.8 272.6 all-reduce.24
  1237.7 35.3 all-reduce.30
  1482.4 51.0 all-reduce.18
  1544.9 272.6 all-reduce.22
  1827.8 35.3 all-reduce.28
  2058.0 51.7 all-reduce.20
where the time goes:
time: 2250 us; the launch traced here: 2240 us
  waiting for transfers between devices  1020 us (45%)
  other arithmetic  612 us (27%)
  local copies, waits for them, and re-layouts  342 us (15%)
  matrix products  234 us (10%)
  between operations  23.2 us (1%)
    psum x9, waiting for transfers between devices, from_root(): return lax.psum(kept, axis)  996 us
    another operation x45, other arithmetic, shards(): cholesky_factor = jnp.linalg.cholesky(mirrored)  239 us
    another operation x7, other arithmetic, shards(): jax.scipy.linalg.solve_triangular(cholesky_factor, flat_cols.T, lower=True)  119 us
    unnamed x1, other arithmetic  92.9 us
    dot_general x1, matrix products, shards(): jnp.einsum('atk,buk->atbu', stacked, stacked_cols, precision=lax.Precisio...  87 us
    unnamed x64, local copies, waits for them, and re-layouts  76.8 us
    another operation x21, matrix products, shards(): jax.scipy.linalg.solve_triangular(cholesky_factor, flat_cols.T, lower=True)  70.8 us
    add x1, other arithmetic, place_rows(): matrix_rows + jnp.einsum('aj,jtx->atx', selector, flat_slots, preferred_e...  67.2 us
  transfers between devices with their start and end apart: 11, of which 10 were waited for; matrix products, arithmetic and copies ran while one was open for 11% of the time, Pallas kernels for 0%

commit v1 on v0

--- a/solution.py
+++ b/solution.py
@@ -8,9 +8,15 @@
 CAP = 2
 
 
+def add_all(x, name):
+    blocks = lax.all_gather(x, name, axis=0, tiled=False)
+    total = blocks.sum(axis=0)
+    return total
+
+
 def from_root(value, axis, source):
     kept = jnp.where(lax.axis_index(axis) == source, value, 0).astype(value.dtype)
-    return lax.psum(kept, axis)
+    return add_all(kept, axis)
 
 
 def slot_ranks(mapping, row_count):

time: 2250 us -> 4290 us (1.91)
  waiting for transfers between devices: 1020 us -> 2860 us
  other arithmetic: 612 us -> 700 us
  local copies, waits for them, and re-layouts: 342 us -> 409 us
    all_gather x0 -> x27, waiting for transfers between devices: none -> 2830 us  [add_all(): blocks = lax.all_gather(x, name, axis=0, tiled=False)]
    psum x9 -> x0, waiting for transfers between devices: 996 us -> none  [from_root(): return lax.psum(kept, axis)]
    reduce_sum x0 -> x27, other arithmetic: none -> 148 us  [add_all(): total = blocks.sum(axis=0)]
    add x1 -> x0, other arithmetic: 67.2 us -> none  [place_rows(): matrix_rows + jnp.einsum('aj,jtx->atx', selector, flat_slots, preferred_e...]
    unnamed x64 -> x37, local copies, waits for them, and re-layouts: 76.8 us -> 129 us
    unnamed x1 -> x2, other arithmetic: 92.9 us -> 100 us
  transfers between devices with their start and end apart: 11 -> 29, of which waited for: 10 -> 25; matrix products, arithmetic and copies ran while one was open for 11% -> 11% of each run, Pallas kernels for 0% -> 0%
where the time goes in v1:
time: 4290 us; the launch traced here: 4280 us
  waiting for transfers between devices  2860 us (67%)
  other arithmetic  700 us (16%)
  local copies, waits for them, and re-layouts  409 us (10%)
  matrix products  276 us (6%)
    all_gather x27, waiting for transfers between devices, add_all(): blocks = lax.all_gather(x, name, axis=0, tiled=False)  2830 us
    another operation x45, other arithmetic, shards(): cholesky_factor = jnp.linalg.cholesky(mirrored)  239 us
    reduce_sum x27, other arithmetic, add_all(): total = blocks.sum(axis=0)  148 us
    unnamed x37, local copies, waits for them, and re-layouts  129 us
    another operation x7, other arithmetic, shards(): jax.scipy.linalg.solve_triangular(cholesky_factor, flat_cols.T, lower=True)  119 us
    unnamed x2, other arithmetic  100 us
    dot_general x1, matrix products, shards(): jnp.einsum('atk,buk->atbu', stacked, stacked_cols, precision=lax.Precisio...  94.6 us
  transfers between devices with their start and end apart: 29, of which 25 were waited for; matrix products, arithmetic and copies ran while one was open for 11% of the time, Pallas kernels for 0%

profile of v1, /device:TPU:0, one launch (start us, length us, event | category | flops | bytes accessed | tf_op | source)
XLA Modules:
  0.0 4276.8 jit_solution(11598522297085850806)
XLA Ops:
  67.8 24.8 all-to-all-done
  98.0 92.7 %reduce.22 = f32[32,128,16,128]{3,2,1,0:T(8,128)} reduce(f32[32,1,128,16,1,128]{5,4,3,2,1,0:T(1,128)} %param.7, f32[]{:T(128)} %broadcast.1047), dimensions={1,4}, to_apply=%param.7.reduce_sub_computation.3 | reduce | bytes 67108864 | tf_op args[0]
  190.7 35.5 reshape.670
  259.4 15.9 fusion.71
  275.3 43.2 %fusion = f32[32,128,2048]{2,0,1:T(8,128)} fusion(f32[32,128,2048]{2,0,1:T(8,128)} %fusion.71, f32[32,128,2048]{2,1,0:T(8,128)} %reshape.670, bf16[8,128,2048]{2,0,1:T(8,128)(2,1)} %reshape.512, s32[16]{0:T(128)S(1)} %multiply_add_fusion.5, s32[16]{0:T(128)S(1)} %get-tuple-element.139, pred[16]{0:T(512)(128)(4,1)S(1)} %get-tuple-element.141), kind=kOutput, calls=%fused_computation.19 | convolution fusion | flops 151004544 | bytes 104857744 | tf_op jit(solution)/shard_map/aj,jtx->atx/dot_general | solution.py:69
  326.1 228.0 %all-gather.67.cloned.1.call-done = f32[256,128,128]{2,0,1:T(8,128)} async-done(((f32[32,128,128]{2,0,1:T(8,128)}), f32[256,128,128]{2,0,1:T(8,128)}) %all-gather.67.cloned.1.call-update) | async-done | bytes 16777232 | tf_op jit(solution)/shard_map/all_gather | solution.py:12
  562.5 219.6 %all-gather.69.cloned.1.call-done = f32[256,128,128]{2,0,1:T(8,128)} async-done(((f32[32,128,128]{2,0,1:T(8,128)}), f32[256,128,128]{2,0,1:T(8,128)}) %all-gather.69.cloned.1.call-update) | async-done | bytes 16777232 | tf_op jit(solution)/shard_map/all_gather | solution.py:12
  791.8 218.3 %all-gather.71.cloned.1.call-done = f32[256,128,128]{2,0,1:T(8,128)} async-done(((f32[32,128,128]{2,0,1:T(8,128)}), f32[256,128,128]{2,0,1:T(8,128)}) %all-gather.71.cloned.1.call-update) | async-done | bytes 16777232 | tf_op jit(solution)/shard_map/all_gather | solution.py:12
  1019.9 218.0 %all-gather.73.cloned.1.call-done = f32[256,128,128]{2,0,1:T(8,128)} async-done(((f32[32,128,128]{2,0,1:T(8,128)}), f32[256,128,128]{2,0,1:T(8,128)}) %all-gather.73.cloned.1.call-update) | async-done | bytes 16777232 | tf_op jit(solution)/shard_map/all_gather | solution.py:12
  1290.1 17.0 all-gather.47.cloned.1.call-done
  1308.4 17.6 all-gather.49.cloned.1.call-done
  1421.4 39.5 custom-call.34
  1556.7 25.7 all-gather.75.cloned.1.call-done
  1601.8 225.5 %all-gather.77.cloned.1.call-done = f32[256,128,128]{2,0,1:T(8,128)} async-done(((f32[32,128,128]{2,0,1:T(8,128)}), f32[256,128,128]{2,0,1:T(8,128)}) %all-gather.77.cloned.1.call-update) | async-done | bytes 16777232 | tf_op jit(solution)/shard_map/all_gather | solution.py:12
  1835.7 219.6 %all-gather.79.cloned.1.call-done = f32[256,128,128]{2,0,1:T(8,128)} async-done(((f32[32,128,128]{2,0,1:T(8,128)}), f32[256,128,128]{2,0,1:T(8,128)}) %all-gather.79.cloned.1.call-update) | async-done | bytes 16777232 | tf_op jit(solution)/shard_map/all_gather | solution.py:12
  2065.1 218.0 %all-gather.81.cloned.1.call-done = f32[256,128,128]{2,0,1:T(8,128)} async-done(((f32[32,128,128]{2,0,1:T(8,128)}), f32[256,128,128]{2,0,1:T(8,128)}) %all-gather.81.cloned.1.call-update) | async-done | bytes 16777232 | tf_op jit(solution)/shard_map/all_gather | solution.py:12
  2292.9 218.2 %all-gather.83.cloned.1.call-done = f32[256,128,128]{2,0,1:T(8,128)} async-done(((f32[32,128,128]{2,0,1:T(8,128)}), f32[256,128,128]{2,0,1:T(8,128)}) %all-gather.83.cloned.1.call-update) | async-done | bytes 16777232 | tf_op jit(solution)/shard_map/all_gather | solution.py:12
  2563.6 16.7 all-gather.55.cloned.1.call-done
  2581.8 17.3 all-gather.57.cloned.1.call-done
  2695.6 39.5 custom-call.38
  2834.1 22.7 all-gather.85.cloned.1.call-done
  2882.0 225.2 %all-gather.87.cloned.1.call-done = f32[256,128,128]{2,0,1:T(8,128)} async-done(((f32[32,128,128]{2,0,1:T(8,128)}), f32[256,128,128]{2,0,1:T(8,128)}) %all-gather.87.cloned.1.call-update) | async-done | bytes 16777232 | tf_op jit(solution)/shard_map/all_gather | solution.py:12
  3115.7 219.4 %all-gather.89.cloned.1.call-done = f32[256,128,128]{2,0,1:T(8,128)} async-done(((f32[32,128,128]{2,0,1:T(8,128)}), f32[256,128,128]{2,0,1:T(8,128)}) %all-gather.89.cloned.1.call-update) | async-done | bytes 16777232 | tf_op jit(solution)/shard_map/all_gather | solution.py:12
  3344.9 218.2 %all-gather.91.cloned.1.call-done = f32[256,128,128]{2,0,1:T(8,128)} async-done(((f32[32,128,128]{2,0,1:T(8,128)}), f32[256,128,128]{2,0,1:T(8,128)}) %all-gather.91.cloned.1.call-update) | async-done | bytes 16777232 | tf_op jit(solution)/shard_map/all_gather | solution.py:12
  3572.9 218.2 %all-gather.93.cloned.1.call-done = f32[256,128,128]{2,0,1:T(8,128)} async-done(((f32[32,128,128]{2,0,1:T(8,128)}), f32[256,128,128]{2,0,1:T(8,128)}) %all-gather.93.cloned.1.call-update) | async-done | bytes 16777232 | tf_op jit(solution)/shard_map/all_gather | solution.py:12
  3843.4 17.0 all-gather.63.cloned.1.call-done
  3861.7 17.4 all-gather.65.cloned.1.call-done
  3974.4 39.7 custom-call.42
  4071.2 27.9 copy.323
  4110.8 18.8 all-gather.95.cloned.1.call-done
  4136.5 94.6 %fusion.2 = f32[32,1,128,16,1,128]{5,2,3,0,4,1:T(8,128)} fusion(f32[32,128,16,128]{3,2,0,1:T(8,128)} %bitcast.353, pred[32,16]{1,0:T(8,128)(4,1)S(1)} %compare_and_fusion, bf16[16,128,512]{2,1,0:T(8,128)(2,1)} %reduce_sum.298, bf16[16,128,512]{2,1,0:T(8,128)(2,1)} %reduce_sum.289, bf16[16,128,512]{2,1,0:T(8,128)(2,1)S(1)} %copy-done.13, ...), kind=kOutput, calls=%fused_computation.22 | convolution fusion | flops 154667057152 | bytes 98566656 | tf_op jit(solution)/shard_map/atk,buk->atbu/dot_general | solution.py:164
  4231.1 38.6 copy.261
  (400 shorter events, 969.2 us)
Async XLA Ops:
  38.7 53.9 %all-to-all-start = ((bf16[4,2,128,2048]{3,1,2,0:T(2,128)(2,1)}), bf16[4,2,128,2048]{3,1,2,0:T(2,128)(2,1)}, u32[]{:S(2)}, u32[]{:S(2)}) async-start(bf16[4,2,128,2048]{3,1,2,0:T(2,128)(2,1)} %copy.202), calls=%async_computation | async-start | bytes 8388608 | tf_op jit(solution)/shard_map/all_to_all | solution.py:120
  92.6 150.3 %all-to-all-start.1 = ((bf16[4,2,128,2048]{3,1,2,0:T(2,128)(2,1)}), bf16[4,2,128,2048]{3,1,2,0:T(2,128)(2,1)}, u32[]{:S(2)}, u32[]{:S(2)}) async-start(bf16[4,2,128,2048]{3,1,2,0:T(2,128)(2,1)} %copy.205), calls=%async_computation.1 | async-start | bytes 8388608 | tf_op jit(solution)/shard_map/all_to_all | solution.py:121
  97.4 456.6 %all-gather.67.cloned.1.call-start = ((), (), s32[]{:S(2)}) async-start(), calls=%async_computation.14 | async-start | bytes 18874368 | tf_op jit(solution)/shard_map/all_gather | solution.py:12
  190.7 35.5 copy-start.14
  323.8 458.3 %all-gather.69.cloned.1.call-start = ((), (), s32[]{:S(2)}) async-start(), calls=%async_computation.15 | async-start | bytes 18874368 | tf_op jit(solution)/shard_map/all_gather | solution.py:12
  324.5 685.5 %all-gather.71.cloned.1.call-start = ((), (), s32[]{:S(2)}) async-start(), calls=%async_computation.16 | async-start | bytes 18874368 | tf_op jit(solution)/shard_map/all_gather | solution.py:12
  325.3 912.6 %all-gather.73.cloned.1.call-start = ((), (), s32[]{:S(2)}) async-start(), calls=%async_computation.17 | async-start | bytes 18874368 | tf_op jit(solution)/shard_map/all_gather | solution.py:12
  325.9 958.3 %all-gather.43.cloned.1.call-start = ((), (), s32[]{:S(2)}) async-start(), calls=%async_computation.2 | async-start | bytes 1310720 | tf_op jit(solution)/shard_map/all_gather | solution.py:12
  1255.5 33.2 all-gather.45.cloned.1.call-start
  1256.3 50.8 %all-gather.47.cloned.1.call-start = ((), (), s32[]{:S(2)}) async-start(), calls=%async_computation.4 | async-start | bytes 1310720 | tf_op jit(solution)/shard_map/all_gather | solution.py:12
  1257.1 68.9 %all-gather.49.cloned.1.call-start = ((), (), s32[]{:S(2)}) async-start(), calls=%async_computation.5 | async-start | bytes 1310720 | tf_op jit(solution)/shard_map/all_gather | solution.py:12
  1257.9 324.5 %all-gather.75.cloned.1.call-start = ((), (), s32[]{:S(2)}) async-start(), calls=%async_computation.18 | async-start | bytes 10485760 | tf_op jit(solution)/shard_map/all_gather | solution.py:12
  1421.4 39.5 copy-start.10
  1524.0 303.2 %all-gather.77.cloned.1.call-start = ((), (), s32[]{:S(2)}) async-start(), calls=%async_computation.19 | async-start | bytes 18874368 | tf_op jit(solution)/shard_map/all_gather | solution.py:12
  1599.5 455.8 %all-gather.79.cloned.1.call-start = ((), (), s32[]{:S(2)}) async-start(), calls=%async_computation.20 | async-start | bytes 18874368 | tf_op jit(solution)/shard_map/all_gather | solution.py:12
  1600.3 682.9 %all-gather.81.cloned.1.call-start = ((), (), s32[]{:S(2)}) async-start(), calls=%async_computation.21 | async-start | bytes 18874368 | tf_op jit(solution)/shard_map/all_gather | solution.py:12
  1600.9 910.3 %all-gather.83.cloned.1.call-start = ((), (), s32[]{:S(2)}) async-start(), calls=%async_computation.22 | async-start | bytes 18874368 | tf_op jit(solution)/shard_map/all_gather | solution.py:12
  1601.6 956.1 %all-gather.51.cloned.1.call-start = ((), (), s32[]{:S(2)}) async-start(), calls=%async_computation.6 | async-start | bytes 1310720 | tf_op jit(solution)/shard_map/all_gather | solution.py:12
  2528.9 33.2 all-gather.53.cloned.1.call-start
  2529.7 50.6 %all-gather.55.cloned.1.call-start = ((), (), s32[]{:S(2)}) async-start(), calls=%async_computation.8 | async-start | bytes 1310720 | tf_op jit(solution)/shard_map/all_gather | solution.py:12
  2530.5 68.5 %all-gather.57.cloned.1.call-start = ((), (), s32[]{:S(2)}) async-start(), calls=%async_computation.9 | async-start | bytes 1310720 | tf_op jit(solution)/shard_map/all_gather | solution.py:12
  2531.3 325.5 %all-gather.85.cloned.1.call-start = ((), (), s32[]{:S(2)}) async-start(), calls=%async_computation.23 | async-start | bytes 10485760 | tf_op jit(solution)/shard_map/all_gather | solution.py:12
  2695.6 39.5 copy-start.11
  2798.5 308.8 %all-gather.87.cloned.1.call-start = ((), (), s32[]{:S(2)}) async-start(), calls=%async_computation.24 | async-start | bytes 18874368 | tf_op jit(solution)/shard_map/all_gather | solution.py:12
  2879.5 455.6 %all-gather.89.cloned.1.call-start = ((), (), s32[]{:S(2)}) async-start(), calls=%async_computation.25 | async-start | bytes 18874368 | tf_op jit(solution)/shard_map/all_gather | solution.py:12
  2880.1 683.0 %all-gather.91.cloned.1.call-start = ((), (), s32[]{:S(2)}) async-start(), calls=%async_computation.26 | async-start | bytes 18874368 | tf_op jit(solution)/shard_map/all_gather | solution.py:12
  2880.8 910.3 %all-gather.93.cloned.1.call-start = ((), (), s32[]{:S(2)}) async-start(), calls=%async_computation.27 | async-start | bytes 18874368 | tf_op jit(solution)/shard_map/all_gather | solution.py:12
  2881.6 956.2 %all-gather.59.cloned.1.call-start = ((), (), s32[]{:S(2)}) async-start(), calls=%async_computation.10 | async-start | bytes 1310720 | tf_op jit(solution)/shard_map/all_gather | solution.py:12
  3808.8 33.2 all-gather.61.cloned.1.call-start
  3809.6 50.8 %all-gather.63.cloned.1.call-start = ((), (), s32[]{:S(2)}) async-start(), calls=%async_computation.12 | async-start | bytes 1310720 | tf_op jit(solution)/shard_map/all_gather | solution.py:12
  3810.4 68.7 %all-gather.65.cloned.1.call-start = ((), (), s32[]{:S(2)}) async-start(), calls=%async_computation.13 | async-start | bytes 1310720 | tf_op jit(solution)/shard_map/all_gather | solution.py:12
  3811.2 318.4 %all-gather.95.cloned.1.call-start = ((), (), s32[]{:S(2)}) async-start(), calls=%async_computation.28 | async-start | bytes 10485760 | tf_op jit(solution)/shard_map/all_gather | solution.py:12
  (12 other events, 86.5 us)
Sparse Core Ops, SparseCore 0:
  323.9 230.0 all-gather.66
  556.2 225.7 all-gather.68
  784.2 225.7 all-gather.70
  1012.1 225.7 all-gather.72
  1255.6 14.8 all-gather.42
  1272.0 16.7 all-gather.44
  1290.3 16.7 all-gather.46
  1309.2 16.7 all-gather.48
  1524.2 58.1 all-gather.74
  1599.7 227.5 all-gather.76
  1829.5 225.7 all-gather.78
  2057.3 225.7 all-gather.80
  2285.3 225.7 all-gather.82
  2529.0 14.8 all-gather.50
  2545.4 16.7 all-gather.52
  2563.6 16.7 all-gather.54
  2582.3 16.7 all-gather.56
  2798.6 58.1 all-gather.84
  2879.6 227.5 all-gather.86
  3109.3 225.7 all-gather.88
  3337.3 225.7 all-gather.90
  3565.3 225.7 all-gather.92
  3808.9 14.8 all-gather.58
  3825.3 16.7 all-gather.60
  3843.6 16.7 all-gather.62
  3862.3 16.7 all-gather.64
  4071.2 58.2 all-gather.94
